TPU v7x, 32 devices: a whole 2x2x4 slice. The times are simulated.
32 devices in a mesh: depth: 2 (over x), map: 16 (over z, y, core).
Axes of the slice: x: 2, y: 2, z: 4, core: 2. Of those that a mesh axis runs over, the one named last changes fastest.
Arguments:
- velocity: float32 [3, 32, 512, 128], P(None, 'depth', 'map'), may hold values from -6 to 6
- stress: float32 [6, 32, 512, 128], P(None, 'depth', 'map'), may hold values from -6 to 6
- region: int32 [32, 512, 128], P('depth', 'map'), may hold values from 0 to 7
- lame_table: float32 [8], replicated, may hold values from 0.2 to 0.5
- shear_table: float32 [8], replicated, may hold values from 0.1 to 0.3
- buoyancy_table: float32 [8], replicated, may hold values from 0.6 to 1.2
- height: float32 [256, 4096], P('depth', 'map'), may hold values from -6 to 6
- discharge: float32 [2, 256, 4096], P(None, 'depth', 'map'), may hold values from -6 to 6
- face_depth: float32 [2, 256, 4096], P(None, 'depth', 'map'), may hold values from 0.5 to 2
- wet: int32 [256, 4096], P('depth', 'map'), may hold values 0 or 1
- seafloor_index: int32 [256, 4096], P('depth', 'map'), may hold values from 0 to 4095
Outputs:
- velocity_out: float32 [3, 32, 512, 128], P(None, 'depth', 'map')
- stress_out: float32 [6, 32, 512, 128], P(None, 'depth', 'map')
- height_out: float32 [256, 4096], P('depth', 'map')
- discharge_out: float32 [2, 256, 4096], P(None, 'depth', 'map')
Inputs may be any that keep to these rules, and one draw needn't show every extreme that they name: `wet`: 1 for a wet ocean cell, 0 for a dry one. `seafloor_index`: index k of the seafloor cell under an ocean cell, among the 32 x 128 crust cells of its own map column, counted row by row.
All inputs are finite; a program needn't handle non-finite values. No bound on the sum of `wet` on one device may be relied on, other than what follows from the above.
Results may differ from a plain program's by a relative error of at most 0.000054.
Values sent between devices are 32-bit elements; how exact they have to be, the bound alone decides.
No kernel may reach another device: no remote copies, remote signals or barrier semaphores. Data moves between devices by JAX's collectives and lax.ppermute only.
A program may use at most 64 MiB of HBM per device.

v0:
```python
import math
import jax
import jax.numpy as jnp
from jax import lax
from jax.sharding import PartitionSpec as P

ITERS = 3
OSTEPS = 2
near_coef = 9.0 / 8.0
far_coef = 1.0 / 24.0
time_step = 0.2
ocean_step = 0.2
gravity = 1.0


def extended(x, sides, width):
    for axis, dim in sides:
        peers, length = (lax.axis_size(axis), x.shape[dim])
        up = [(i, (i + 1) % peers) for i in range(peers - 1)]
        down = [(j, i) for i, j in up]
        last = lax.slice_in_dim(x, length - width, length, axis=dim)
        leading = lax.slice_in_dim(x, 0, width, axis=dim)
        before = lax.ppermute(last, axis, up)
        after = lax.ppermute(leading, axis, down)
        x = jnp.concatenate([before, x, after], axis=dim)
    return x


def broadcast(x, axis, root):
    mine = lax.axis_index(axis) == root
    return lax.psum(jnp.where(mine, x, jnp.zeros_like(x)), axis)


def passed_along(x, axis, by):
    peers = lax.axis_size(axis)
    pairs = [(i, i + by) for i in range(peers) if 0 <= i + by < peers]
    return lax.ppermute(x, axis, pairs)


def cells(padded, axis, offset, count):
    return lax.slice_in_dim(padded, offset, offset + count, axis=axis)


def forward_diff(padded, axis):
    count = padded.shape[axis] - 4
    return near_coef * (
        cells(padded, axis, 3, count) - cells(padded, axis, 2, count)
    ) - far_coef * (cells(padded, axis, 4, count) - cells(padded, axis, 1, count))


def backward_diff(padded, axis):
    count = padded.shape[axis] - 4
    return near_coef * (
        cells(padded, axis, 2, count) - cells(padded, axis, 1, count)
    ) - far_coef * (cells(padded, axis, 3, count) - cells(padded, axis, 0, count))


def forward_y(field):
    return near_coef * (jnp.roll(field, -1, 2) - field) - far_coef * (
        jnp.roll(field, -2, 2) - jnp.roll(field, 1, 2)
    )


def backward_y(field):
    return near_coef * (field - jnp.roll(field, 1, 2)) - far_coef * (
        jnp.roll(field, -1, 2) - jnp.roll(field, 2, 2)
    )


def lookup(region, table):
    total = jnp.zeros(region.shape, jnp.float32)
    for value in range(table.shape[0]):
        total = total + jnp.where(region == value, table[value], 0.0)
    return total


def seafloor_pick(tiles, seafloor_index):
    tile_rows = tiles.shape[1]
    tile_cols = tiles.shape[2]
    ocean_rows = seafloor_index.shape[0]
    ocean_cols = seafloor_index.shape[1]
    group = math.gcd(ocean_rows, 8)
    table = jnp.transpose(tiles, (1, 0, 2)).reshape(tile_rows, 2 * tile_cols)
    row_ids = lax.broadcasted_iota(jnp.int32, (1, 1, tile_rows), 2)
    col_ids = lax.broadcasted_iota(jnp.int32, (1, 1, tile_cols), 2)

    def one_block(indices):
        upper = indices // tile_cols
        lower = indices % tile_cols
        onehot = (upper[:, :, None] == row_ids).astype(jnp.float32)
        picked = jnp.einsum("rck,kn->rcn", onehot, table, precision=lax.Precision.HIGHEST)
        chosen = lower[:, :, None] == col_ids
        first = jnp.sum(jnp.where(chosen, picked[:, :, :tile_cols], 0.0), axis=2)
        second = jnp.sum(jnp.where(chosen, picked[:, :, tile_cols:], 0.0), axis=2)
        return jnp.stack([first, second])

    blocks = seafloor_index.reshape(ocean_rows // group, group, ocean_cols)
    result = lax.map(one_block, blocks)
    result = jnp.transpose(result, (1, 0, 2, 3)).reshape(2, ocean_rows, ocean_cols)
    return (result[0], result[1])


def per_device(
    velocity,
    stress,
    region,
    lame_table,
    shear_table,
    buoyancy_table,
    height,
    discharge,
    face_depth,
    wet,
    seafloor_index,
):
    lame = lookup(region, lame_table)
    shear = lookup(region, shear_table)
    buoyancy = lookup(region, buoyancy_table)
    speeds = velocity
    forces = stress
    lift = jnp.zeros((velocity.shape[2], velocity.shape[3]), jnp.float32)
    for turn in range(ITERS):
        map_part = extended(forces[0:3], (("map", 2),), 2)
        depth_part = extended(forces[2:5], (("depth", 1),), 2)
        speed_x = speeds[0] + time_step * buoyancy * (
            forward_diff(map_part[0], 1) + backward_y(forces[1]) + backward_diff(depth_part[0], 0)
        )
        speed_y = speeds[1] + time_step * buoyancy * (
            backward_diff(map_part[1], 1) + forward_y(forces[5]) + backward_diff(depth_part[1], 0)
        )
        speed_z = speeds[2] + time_step * buoyancy * (
            backward_diff(map_part[2], 1) + backward_y(forces[3]) + forward_diff(depth_part[2], 0)
        )
        speeds = jnp.stack([speed_x, speed_y, speed_z])
        lift = lift + time_step * speed_z[0]
        beside_all = extended(speeds, (("depth", 1), ("map", 2)), 2)
        speed_map = beside_all[:, 2:-2]
        speed_depth = beside_all[:, :, 2:-2]
        strain_x = backward_diff(speed_map[0], 1)
        strain_y = backward_y(speed_y)
        strain_z = backward_diff(speed_depth[2], 0)
        spread = strain_x + strain_y + strain_z
        forces = jnp.stack(
            [
                forces[0] + time_step * (lame * spread + 2.0 * shear * strain_x),
                forces[1]
                + time_step * shear * (forward_y(speed_x) + forward_diff(speed_map[1], 1)),
                forces[2]
                + time_step
                * shear
                * (forward_diff(speed_depth[0], 0) + forward_diff(speed_map[2], 1)),
                forces[3]
                + time_step * shear * (forward_diff(speed_depth[1], 0) + forward_y(speed_z)),
                forces[4] + time_step * (lame * spread + 2.0 * shear * strain_z),
                forces[5] + time_step * (lame * spread + 2.0 * shear * strain_y),
            ]
        )
    tiles = broadcast(jnp.stack([lift, speeds[2][0]]), "depth", 0)
    lift_at, rate_at = seafloor_pick(tiles, seafloor_index)
    wetness = wet.astype(jnp.float32)
    level = wetness * (height + lift_at)
    source = wetness * rate_at
    east_pair = passed_along(jnp.stack([level[:, :1], wetness[:, :1]]), "map", -1)
    north_pair = passed_along(jnp.stack([level[:1, :], wetness[:1, :]]), "depth", -1)
    wet_east = jnp.concatenate([wetness[:, 1:], east_pair[1]], axis=1)
    wet_north = jnp.concatenate([wetness[1:, :], north_pair[1]], axis=0)
    mask_x = wetness * wet_east
    mask_y = wetness * wet_north
    depth_x = face_depth[0] * mask_x
    depth_y = face_depth[1] * mask_y
    flux_x = discharge[0] * mask_x
    flux_y = discharge[1] * mask_y
    for turn in range(OSTEPS):
        if turn == 0:
            east_col = east_pair[0]
            north_row = north_pair[0]
        else:
            east_col = passed_along(level[:, :1], "map", -1)
            north_row = passed_along(level[:1, :], "depth", -1)
        level_east = jnp.concatenate([level[:, 1:], east_col], axis=1)
        level_north = jnp.concatenate([level[1:, :], north_row], axis=0)
        flux_x = flux_x - ocean_step * gravity * depth_x * (level_east - level)
        flux_y = flux_y - ocean_step * gravity * depth_y * (level_north - level)
        west_col = passed_along(flux_x[:, -1:], "map", 1)
        south_row = passed_along(flux_y[-1:, :], "depth", 1)
        flux_west = jnp.concatenate([west_col, flux_x[:, :-1]], axis=1)
        flux_south = jnp.concatenate([south_row, flux_y[:-1, :]], axis=0)
        level = (
            level
            - ocean_step * wetness * (flux_x - flux_west + (flux_y - flux_south))
            + ocean_step * source
        )
    return (speeds, forces, level, jnp.stack([flux_x, flux_y]))


def solution(mesh):
    return jax.shard_map(
        per_device,
        mesh=mesh,
        in_specs=(
            P(None, "depth", "map", None),
            P(None, "depth", "map", None),
            P("depth", "map", None),
            P(),
            P(),
            P(),
            P("depth", "map"),
            P(None, "depth", "map"),
            P(None, "depth", "map"),
            P("depth", "map"),
            P("depth", "map"),
        ),
        out_specs=(
            P(None, "depth", "map", None),
            P(None, "depth", "map", None),
            P("depth", "map"),
            P(None, "depth", "map"),
        ),
        check_vma=False,
    )
```

profile of v0, /device:TPU:7, one launch (start us, length us, event | category | flops | bytes accessed | tf_op | source)
XLA Modules:
  0.0 251.1 jit_solution(1492550919271240779)
XLA Ops:
  2.3 3.7 %collective-permute-start = (f32[3,16,2,128]{3,2,1,0:T(2,128)}, f32[3,16,2,128]{3,2,1,0:T(2,128)}, u32[]{:S(2)}, u32[]{:S(2)}) collective-permute-start(f32[3,16,2,128]{3,2,1,0:T(2,128)} %get-tuple-element.138), channel_id=1, source_target_pairs={{0,1},{1,2},{2,3},{3,4},{4,5},{5,6},{6,7},{7,8},{8,9},{9,10},{10,1... | collective-permute-start | bytes 147464 | tf_op jit(solution)/shard_map/ppermute | solution.py:23
  6.0 1.9 collective-permute-start.1
  10.9 4.8 %collective-permute-start.3 = (f32[3,2,32,128]{3,2,1,0:T(8,128)}, f32[3,2,32,128]{3,2,1,0:T(8,128)}, u32[]{:S(2)}, u32[]{:S(2)}) collective-permute-start(f32[3,2,32,128]{3,2,1,0:T(8,128)} %get-tuple-element.143), channel_id=1, source_target_pairs={{16,0},{17,1},{18,2},{19,3},{20,4},{21,5},{22,6},{23,7},{24,8},{25... | collective-permute-start | bytes 294920 | tf_op jit(solution)/shard_map/ppermute | solution.py:24
  30.2 6.6 %fusion.30 = (f32[16,32,128]{2,1,0:T(8,128)S(1)}, f32[16,32,128]{2,1,0:T(8,128)S(1)}, pred[16,32,128]{2,1,0:T(8,128)(4,1)S(1)}, pred[16,32,128]{2,1,0:T(8,128)(4...) fusion(f32[3,16,32,128]{3,2,1,0:T(8,128)S(1)} %copy-done.1, ...), kind=kLoop, calls=%fused_computation.102 | loop fusion | flops 3211264 | bytes 4915232 | tf_op jit(solution)/shard_map/add | solution.py:125
  42.1 4.0 %collective-permute-start.5 = (f32[3,2,32,128]{3,2,1,0:T(8,128)S(1)}, f32[3,2,32,128]{3,2,1,0:T(8,128)S(1)}, u32[]{:S(2)}, u32[]{:S(2)}) collective-permute-start(f32[3,2,32,128]{3,2,1,0:T(8,128)S(1)} %get-tuple-element.190), channel_id=1, source_target_pairs={{16,0},{17,1},{18,2},{19,3},{20,4},{21,5},{22,6},{23,7},{24,8},{25... | collective-permute-start | bytes 294920 | tf_op jit(solution)/shard_map/ppermute | solution.py:24
  47.8 6.2 %collective-permute-start.6 = (f32[3,20,2,128]{3,2,1,0:T(2,128)S(1)}, f32[3,20,2,128]{3,2,1,0:T(2,128)S(1)}, u32[]{:S(2)}, u32[]{:S(2)}) collective-permute-start(f32[3,20,2,128]{3,2,1,0:T(2,128)S(1)} %get-tuple-element.160), channel_id=1, source_target_pairs={{0,1},{1,2},{2,3},{3,4},{4,5},{5,6},{6,7},{7,8},{8,9},{9,10},{10,1... | collective-permute-start | bytes 184328 | tf_op jit(solution)/shard_map/ppermute | solution.py:23
  54.0 1.9 collective-permute-start.7
  56.2 4.2 %collective-permute-done.7 = f32[3,20,2,128]{3,2,1,0:T(2,128)S(1)} collective-permute-done((f32[3,20,2,128]{3,2,1,0:T(2,128)S(1)}, f32[3,20,2,128]{3,2,1,0:T(2,128)S(1)}, u32[]{:S(2)}, u32[]{:S(2)}) %collective-permute-start.7) | collective-permute-done | bytes 61472 | tf_op jit(solution)/shard_map/ppermute | solution.py:24
  60.5 10.9 %multiply_add_fusion.3 = (f32[16,32,128]{2,1,0:T(8,128)S(1)}, f32[16,32,128]{2,1,0:T(8,128)S(1)}, f32[16,32,128]{2,1,0:T(8,128)S(1)}, f32[16,32,128]{2,1,0:T(8,1...) fusion(f32[6,16,32,128]{3,2,1,0:T(8,128)S(1)} %copy-done, ...), kind=kLoop, calls=%fused_computation.482 | loop fusion | flops 3670016 | bytes 5505088 | tf_op jit(solution)/shard_map/add | solution.py:155
  73.5 1.9 collective-permute-start.8
  75.4 2.4 collective-permute-start.9
  79.5 4.0 %collective-permute-start.11 = (f32[3,2,32,128]{3,2,1,0:T(8,128)S(1)}, f32[3,2,32,128]{3,2,1,0:T(8,128)S(1)}, u32[]{:S(2)}, u32[]{:S(2)}) collective-permute-start(f32[3,2,32,128]{3,2,1,0:T(8,128)S(1)} %get-tuple-element.185), channel_id=1, source_target_pairs={{16,0},{17,1},{18,2},{19,3},{20,4},{21,5},{22,6},{23,7},{24,8},{25... | collective-permute-start | bytes 294920 | tf_op jit(solution)/shard_map/ppermute | solution.py:24
  88.9 4.1 %collective-permute-start.13 = (f32[3,2,32,128]{3,2,1,0:T(8,128)S(1)}, f32[3,2,32,128]{3,2,1,0:T(8,128)S(1)}, u32[]{:S(2)}, u32[]{:S(2)}) collective-permute-start(f32[3,2,32,128]{3,2,1,0:T(8,128)S(1)} %get-tuple-element.180), channel_id=1, source_target_pairs={{16,0},{17,1},{18,2},{19,3},{20,4},{21,5},{22,6},{23,7},{24,8},{25... | collective-permute-start | bytes 294920 | tf_op jit(solution)/shard_map/ppermute | solution.py:24
  94.7 5.9 %collective-permute-start.14 = (f32[3,20,2,128]{3,2,1,0:T(2,128)S(1)}, f32[3,20,2,128]{3,2,1,0:T(2,128)S(1)}, u32[]{:S(2)}, u32[]{:S(2)}) collective-permute-start(f32[3,20,2,128]{3,2,1,0:T(2,128)S(1)} %get-tuple-element.155), channel_id=1, source_target_pairs={{0,1},{1,2},{2,3},{3,4},{4,5},{5,6},{6,7},{7,8},{8,9},{9,10},{10,1... | collective-permute-start | bytes 184328 | tf_op jit(solution)/shard_map/ppermute | solution.py:23
  100.6 2.1 collective-permute-start.15
  104.0 3.1 %collective-permute-done.15 = f32[3,20,2,128]{3,2,1,0:T(2,128)S(1)} collective-permute-done((f32[3,20,2,128]{3,2,1,0:T(2,128)S(1)}, f32[3,20,2,128]{3,2,1,0:T(2,128)S(1)}, u32[]{:S(2)}, u32[]{:S(2)}) %collective-permute-start.15) | collective-permute-done | bytes 61472 | tf_op jit(solution)/shard_map/ppermute | solution.py:24
  112.0 1.9 collective-permute-start.16
  113.9 2.4 collective-permute-start.17
  119.3 4.0 %collective-permute-start.19 = (f32[3,2,32,128]{3,2,1,0:T(8,128)S(1)}, f32[3,2,32,128]{3,2,1,0:T(8,128)S(1)}, u32[]{:S(2)}, u32[]{:S(2)}) collective-permute-start(f32[3,2,32,128]{3,2,1,0:T(8,128)S(1)} %get-tuple-element.175), channel_id=1, source_target_pairs={{16,0},{17,1},{18,2},{19,3},{20,4},{21,5},{22,6},{23,7},{24,8},{25... | collective-permute-start | bytes 294920 | tf_op jit(solution)/shard_map/ppermute | solution.py:24
  126.7 7.3 %psum.7 = f32[32,256]{1,0:T(8,128)S(1)} all-reduce(f32[32,256]{1,0:T(8,128)S(1)} %copy_bitcast_fusion), channel_id=1, replica_groups=mesh['depth'=2,'map'=16] {'depth'}, use_global_device_ids=true, to_apply=%region_0.1 | all-reduce | flops 8192 | bytes 65536 | tf_op jit(solution)/shard_map/psum | solution.py:31
  134.0 52.3 %while.13 = (s32[]{:T(128)}, f32[16,2,8,256]{3,2,1,0:T(8,128)}, s32[16,8,256]{2,1,0:T(8,128)}, f32[32,256]{1,0:T(8,128)S(1)}, s32[]{:T(128)}) while((s32[]{:T(128)}, f32[16,2,8,256]{3,2,1,0:T(8,128)}, s32[16,8,256]{2,1,0:T(8,128)}, f32[32,256]{1,0:T(8,128)S(1)}, s32[]{:T(128)}) %tuple.162), condition=%wide.region_4.5_spmd.clone, body=%wide.region_1.4_spmd.clone.sunk | while | flops 202754048 | bytes 4330053 | solution.py:98
  187.4 2.4 fusion.105
  196.6 5.0 %collective-permute-start.24 = (f32[2,128,1]{1,2,0:T(1,128)S(1)}, f32[2,128,1]{1,2,0:T(1,128)S(1)}, u32[]{:S(2)}, u32[]{:S(2)}) collective-permute-start(f32[2,128,1]{1,2,0:T(1,128)S(1)} %pad_maximum_fusion.64), channel_id=1, source_target_pairs={{1,0},{2,1},{3,2},{4,3},{5,4},{6,5},{7,6},{8,7},{9,8},{10,9},{11,1... | collective-permute-start | bytes 3080 | tf_op jit(solution)/shard_map/ppermute | solution.py:37
  206.8 4.6 %collective-permute-start.25 = (f32[128,1]{1,0:T(8,128)S(1)}, f32[128,1]{1,0:T(8,128)S(1)}, u32[]{:S(2)}, u32[]{:S(2)}) collective-permute-start(f32[128,1]{1,0:T(8,128)S(1)} %slice.2012), channel_id=1, source_target_pairs={{0,1},{1,2},{2,3},{3,4},{4,5},{5,6},{6,7},{7,8},{8,9},{9,10},{10,1... | collective-permute-start | bytes 1544 | tf_op jit(solution)/shard_map/ppermute | solution.py:37
  212.8 2.9 %collective-permute-done.27 = f32[1,256]{1,0:T(1,128)S(1)} collective-permute-done((f32[1,256]{1,0:T(1,128)S(1)}, f32[1,256]{1,0:T(1,128)S(1)}, u32[]{:S(2)}, u32[]{:S(2)}) %collective-permute-start.27) | collective-permute-done | bytes 1056 | tf_op jit(solution)/shard_map/ppermute | solution.py:37
  215.9 2.1 collective-permute-start.28
  221.4 4.0 %collective-permute-start.21 = (f32[3,2,32,128]{3,2,1,0:T(8,128)S(1)}, f32[3,2,32,128]{3,2,1,0:T(8,128)S(1)}, u32[]{:S(2)}, u32[]{:S(2)}) collective-permute-start(f32[3,2,32,128]{3,2,1,0:T(8,128)S(1)} %get-tuple-element.170), channel_id=1, source_target_pairs={{16,0},{17,1},{18,2},{19,3},{20,4},{21,5},{22,6},{23,7},{24,8},{25... | collective-permute-start | bytes 294920 | tf_op jit(solution)/shard_map/ppermute | solution.py:24
  225.8 5.4 %collective-permute-start.29 = (f32[128,1]{1,0:T(8,128)S(1)}, f32[128,1]{1,0:T(8,128)S(1)}, u32[]{:S(2)}, u32[]{:S(2)}) collective-permute-start(f32[128,1]{1,0:T(8,128)S(1)} %slice.2025), channel_id=1, source_target_pairs={{0,1},{1,2},{2,3},{3,4},{4,5},{5,6},{6,7},{7,8},{8,9},{9,10},{10,1... | collective-permute-start | bytes 1544 | tf_op jit(solution)/shard_map/ppermute | solution.py:37
  233.2 2.3 collective-permute-done.31
  236.3 3.1 %collective-permute-start.22 = (f32[3,20,2,128]{3,2,1,0:T(2,128)S(1)}, f32[3,20,2,128]{3,2,1,0:T(2,128)S(1)}, u32[]{:S(2)}, u32[]{:S(2)}) collective-permute-start(f32[3,20,2,128]{3,2,1,0:T(2,128)S(1)} %get-tuple-element.150), channel_id=1, source_target_pairs={{0,1},{1,2},{2,3},{3,4},{4,5},{5,6},{6,7},{7,8},{8,9},{9,10},{10,1... | collective-permute-start | bytes 184328 | tf_op jit(solution)/shard_map/ppermute | solution.py:23
  239.5 2.1 collective-permute-start.23
  241.8 4.2 %collective-permute-done.23 = f32[3,20,2,128]{3,2,1,0:T(2,128)S(1)} collective-permute-done((f32[3,20,2,128]{3,2,1,0:T(2,128)S(1)}, f32[3,20,2,128]{3,2,1,0:T(2,128)S(1)}, u32[]{:S(2)}, u32[]{:S(2)}) %collective-permute-start.23) | collective-permute-done | bytes 61472 | tf_op jit(solution)/shard_map/ppermute | solution.py:24
  (384 shorter events, 127.0 us)
Async XLA Ops:
  2.3 25.8 %collective-permute-start = (f32[3,16,2,128]{3,2,1,0:T(2,128)}, f32[3,16,2,128]{3,2,1,0:T(2,128)}, u32[]{:S(2)}, u32[]{:S(2)}) collective-permute-start(f32[3,16,2,128]{3,2,1,0:T(2,128)} %get-tuple-element.138), channel_id=1, source_target_pairs={{0,1},{1,2},{2,3},{3,4},{4,5},{5,6},{6,7},{7,8},{8,9},{9,10},{10,1... | collective-permute-start | bytes 147464 | tf_op jit(solution)/shard_map/ppermute | solution.py:23
  6.0 22.1 %collective-permute-start.1 = (f32[3,16,2,128]{3,2,1,0:T(2,128)}, f32[3,16,2,128]{3,2,1,0:T(2,128)}, u32[]{:S(2)}, u32[]{:S(2)}) collective-permute-start(f32[3,16,2,128]{3,2,1,0:T(2,128)} %get-tuple-element.139), channel_id=1, source_target_pairs={{1,0},{2,1},{3,2},{4,3},{5,4},{6,5},{7,6},{8,7},{9,8},{10,9},{11,1... | collective-permute-start | bytes 147464 | tf_op jit(solution)/shard_map/ppermute | solution.py:24
  9.6 19.8 %collective-permute-start.2 = (f32[3,2,32,128]{3,2,1,0:T(8,128)}, f32[3,2,32,128]{3,2,1,0:T(8,128)S(1)}, u32[]{:S(2)}, u32[]{:S(2)}) collective-permute-start(f32[3,2,32,128]{3,2,1,0:T(8,128)} %get-tuple-element.142), channel_id=1, source_target_pairs={{0,16},{1,17},{2,18},{3,19},{4,20},{5,21},{6,22},{7,23},{8,24},{9,... | collective-permute-start | bytes 294920 | tf_op jit(solution)/shard_map/ppermute | solution.py:23
  10.9 18.5 %collective-permute-start.3 = (f32[3,2,32,128]{3,2,1,0:T(8,128)}, f32[3,2,32,128]{3,2,1,0:T(8,128)}, u32[]{:S(2)}, u32[]{:S(2)}) collective-permute-start(f32[3,2,32,128]{3,2,1,0:T(8,128)} %get-tuple-element.143), channel_id=1, source_target_pairs={{16,0},{17,1},{18,2},{19,3},{20,4},{21,5},{22,6},{23,7},{24,8},{25... | collective-permute-start | bytes 294920 | tf_op jit(solution)/shard_map/ppermute | solution.py:24
  40.8 5.9 %collective-permute-start.4 = (f32[3,2,32,128]{3,2,1,0:T(8,128)S(1)}, f32[3,2,32,128]{3,2,1,0:T(8,128)S(1)}, u32[]{:S(2)}, u32[]{:S(2)}) collective-permute-start(f32[3,2,32,128]{3,2,1,0:T(8,128)S(1)} %get-tuple-element.189), channel_id=1, source_target_pairs={{0,16},{1,17},{2,18},{3,19},{4,20},{5,21},{6,22},{7,23},{8,24},{9,... | collective-permute-start | bytes 294920 | tf_op jit(solution)/shard_map/ppermute | solution.py:23
  42.1 5.6 %collective-permute-start.5 = (f32[3,2,32,128]{3,2,1,0:T(8,128)S(1)}, f32[3,2,32,128]{3,2,1,0:T(8,128)S(1)}, u32[]{:S(2)}, u32[]{:S(2)}) collective-permute-start(f32[3,2,32,128]{3,2,1,0:T(8,128)S(1)} %get-tuple-element.190), channel_id=1, source_target_pairs={{16,0},{17,1},{18,2},{19,3},{20,4},{21,5},{22,6},{23,7},{24,8},{25... | collective-permute-start | bytes 294920 | tf_op jit(solution)/shard_map/ppermute | solution.py:24
  47.8 8.4 %collective-permute-start.6 = (f32[3,20,2,128]{3,2,1,0:T(2,128)S(1)}, f32[3,20,2,128]{3,2,1,0:T(2,128)S(1)}, u32[]{:S(2)}, u32[]{:S(2)}) collective-permute-start(f32[3,20,2,128]{3,2,1,0:T(2,128)S(1)} %get-tuple-element.160), channel_id=1, source_target_pairs={{0,1},{1,2},{2,3},{3,4},{4,5},{5,6},{6,7},{7,8},{8,9},{9,10},{10,1... | collective-permute-start | bytes 184328 | tf_op jit(solution)/shard_map/ppermute | solution.py:23
  54.0 6.4 %collective-permute-start.7 = (f32[3,20,2,128]{3,2,1,0:T(2,128)S(1)}, f32[3,20,2,128]{3,2,1,0:T(2,128)S(1)}, u32[]{:S(2)}, u32[]{:S(2)}) collective-permute-start(f32[3,20,2,128]{3,2,1,0:T(2,128)S(1)} %get-tuple-element.161), channel_id=1, source_target_pairs={{1,0},{2,1},{3,2},{4,3},{5,4},{6,5},{7,6},{8,7},{9,8},{10,9},{11,1... | collective-permute-start | bytes 184328 | tf_op jit(solution)/shard_map/ppermute | solution.py:24
  73.5 10.1 %collective-permute-start.8 = (f32[3,16,2,128]{3,2,1,0:T(2,128)S(1)}, f32[3,16,2,128]{3,2,1,0:T(2,128)S(1)}, u32[]{:S(2)}, u32[]{:S(2)}) collective-permute-start(f32[3,16,2,128]{3,2,1,0:T(2,128)S(1)} %get-tuple-element.181), channel_id=1, source_target_pairs={{0,1},{1,2},{2,3},{3,4},{4,5},{5,6},{6,7},{7,8},{8,9},{9,10},{10,1... | collective-permute-start | bytes 147464 | tf_op jit(solution)/shard_map/ppermute | solution.py:23
  75.4 8.2 %collective-permute-start.9 = (f32[3,16,2,128]{3,2,1,0:T(2,128)S(1)}, f32[3,16,2,128]{3,2,1,0:T(2,128)S(1)}, u32[]{:S(2)}, u32[]{:S(2)}) collective-permute-start(f32[3,16,2,128]{3,2,1,0:T(2,128)S(1)} %get-tuple-element.182), channel_id=1, source_target_pairs={{1,0},{2,1},{3,2},{4,3},{5,4},{6,5},{7,6},{8,7},{9,8},{10,9},{11,1... | collective-permute-start | bytes 147464 | tf_op jit(solution)/shard_map/ppermute | solution.py:24
  78.2 6.3 %collective-permute-start.10 = (f32[3,2,32,128]{3,2,1,0:T(8,128)S(1)}, f32[3,2,32,128]{3,2,1,0:T(8,128)S(1)}, u32[]{:S(2)}, u32[]{:S(2)}) collective-permute-start(f32[3,2,32,128]{3,2,1,0:T(8,128)S(1)} %get-tuple-element.186), channel_id=1, source_target_pairs={{0,16},{1,17},{2,18},{3,19},{4,20},{5,21},{6,22},{7,23},{8,24},{9,... | collective-permute-start | bytes 294920 | tf_op jit(solution)/shard_map/ppermute | solution.py:23
  79.5 5.9 %collective-permute-start.11 = (f32[3,2,32,128]{3,2,1,0:T(8,128)S(1)}, f32[3,2,32,128]{3,2,1,0:T(8,128)S(1)}, u32[]{:S(2)}, u32[]{:S(2)}) collective-permute-start(f32[3,2,32,128]{3,2,1,0:T(8,128)S(1)} %get-tuple-element.185), channel_id=1, source_target_pairs={{16,0},{17,1},{18,2},{19,3},{20,4},{21,5},{22,6},{23,7},{24,8},{25... | collective-permute-start | bytes 294920 | tf_op jit(solution)/shard_map/ppermute | solution.py:24
  87.6 6.0 %collective-permute-start.12 = (f32[3,2,32,128]{3,2,1,0:T(8,128)S(1)}, f32[3,2,32,128]{3,2,1,0:T(8,128)S(1)}, u32[]{:S(2)}, u32[]{:S(2)}) collective-permute-start(f32[3,2,32,128]{3,2,1,0:T(8,128)S(1)} %get-tuple-element.179), channel_id=1, source_target_pairs={{0,16},{1,17},{2,18},{3,19},{4,20},{5,21},{6,22},{7,23},{8,24},{9,... | collective-permute-start | bytes 294920 | tf_op jit(solution)/shard_map/ppermute | solution.py:23
  88.9 5.7 %collective-permute-start.13 = (f32[3,2,32,128]{3,2,1,0:T(8,128)S(1)}, f32[3,2,32,128]{3,2,1,0:T(8,128)S(1)}, u32[]{:S(2)}, u32[]{:S(2)}) collective-permute-start(f32[3,2,32,128]{3,2,1,0:T(8,128)S(1)} %get-tuple-element.180), channel_id=1, source_target_pairs={{16,0},{17,1},{18,2},{19,3},{20,4},{21,5},{22,6},{23,7},{24,8},{25... | collective-permute-start | bytes 294920 | tf_op jit(solution)/shard_map/ppermute | solution.py:24
  94.7 9.3 %collective-permute-start.14 = (f32[3,20,2,128]{3,2,1,0:T(2,128)S(1)}, f32[3,20,2,128]{3,2,1,0:T(2,128)S(1)}, u32[]{:S(2)}, u32[]{:S(2)}) collective-permute-start(f32[3,20,2,128]{3,2,1,0:T(2,128)S(1)} %get-tuple-element.155), channel_id=1, source_target_pairs={{0,1},{1,2},{2,3},{3,4},{4,5},{5,6},{6,7},{7,8},{8,9},{9,10},{10,1... | collective-permute-start | bytes 184328 | tf_op jit(solution)/shard_map/ppermute | solution.py:23
  100.6 6.4 %collective-permute-start.15 = (f32[3,20,2,128]{3,2,1,0:T(2,128)S(1)}, f32[3,20,2,128]{3,2,1,0:T(2,128)S(1)}, u32[]{:S(2)}, u32[]{:S(2)}) collective-permute-start(f32[3,20,2,128]{3,2,1,0:T(2,128)S(1)} %get-tuple-element.156), channel_id=1, source_target_pairs={{1,0},{2,1},{3,2},{4,3},{5,4},{6,5},{7,6},{8,7},{9,8},{10,9},{11,1... | collective-permute-start | bytes 184328 | tf_op jit(solution)/shard_map/ppermute | solution.py:24
  112.0 11.4 %collective-permute-start.16 = (f32[3,16,2,128]{3,2,1,0:T(2,128)S(1)}, f32[3,16,2,128]{3,2,1,0:T(2,128)S(1)}, u32[]{:S(2)}, u32[]{:S(2)}) collective-permute-start(f32[3,16,2,128]{3,2,1,0:T(2,128)S(1)} %get-tuple-element.171), channel_id=1, source_target_pairs={{0,1},{1,2},{2,3},{3,4},{4,5},{5,6},{6,7},{7,8},{8,9},{9,10},{10,1... | collective-permute-start | bytes 147464 | tf_op jit(solution)/shard_map/ppermute | solution.py:23
  113.9 9.5 %collective-permute-start.17 = (f32[3,16,2,128]{3,2,1,0:T(2,128)S(1)}, f32[3,16,2,128]{3,2,1,0:T(2,128)S(1)}, u32[]{:S(2)}, u32[]{:S(2)}) collective-permute-start(f32[3,16,2,128]{3,2,1,0:T(2,128)S(1)} %get-tuple-element.172), channel_id=1, source_target_pairs={{1,0},{2,1},{3,2},{4,3},{5,4},{6,5},{7,6},{8,7},{9,8},{10,9},{11,1... | collective-permute-start | bytes 147464 | tf_op jit(solution)/shard_map/ppermute | solution.py:24
  118.1 6.4 %collective-permute-start.18 = (f32[3,2,32,128]{3,2,1,0:T(8,128)S(1)}, f32[3,2,32,128]{3,2,1,0:T(8,128)S(1)}, u32[]{:S(2)}, u32[]{:S(2)}) collective-permute-start(f32[3,2,32,128]{3,2,1,0:T(8,128)S(1)} %get-tuple-element.176), channel_id=1, source_target_pairs={{0,16},{1,17},{2,18},{3,19},{4,20},{5,21},{6,22},{7,23},{8,24},{9,... | collective-permute-start | bytes 294920 | tf_op jit(solution)/shard_map/ppermute | solution.py:23
  119.3 5.9 %collective-permute-start.19 = (f32[3,2,32,128]{3,2,1,0:T(8,128)S(1)}, f32[3,2,32,128]{3,2,1,0:T(8,128)S(1)}, u32[]{:S(2)}, u32[]{:S(2)}) collective-permute-start(f32[3,2,32,128]{3,2,1,0:T(8,128)S(1)} %get-tuple-element.175), channel_id=1, source_target_pairs={{16,0},{17,1},{18,2},{19,3},{20,4},{21,5},{22,6},{23,7},{24,8},{25... | collective-permute-start | bytes 294920 | tf_op jit(solution)/shard_map/ppermute | solution.py:24
  196.6 8.2 %collective-permute-start.24 = (f32[2,128,1]{1,2,0:T(1,128)S(1)}, f32[2,128,1]{1,2,0:T(1,128)S(1)}, u32[]{:S(2)}, u32[]{:S(2)}) collective-permute-start(f32[2,128,1]{1,2,0:T(1,128)S(1)} %pad_maximum_fusion.64), channel_id=1, source_target_pairs={{1,0},{2,1},{3,2},{4,3},{5,4},{6,5},{7,6},{8,7},{9,8},{10,9},{11,1... | collective-permute-start | bytes 3080 | tf_op jit(solution)/shard_map/ppermute | solution.py:37
  203.1 2.4 collective-permute-start.26
  206.8 6.0 %collective-permute-start.25 = (f32[128,1]{1,0:T(8,128)S(1)}, f32[128,1]{1,0:T(8,128)S(1)}, u32[]{:S(2)}, u32[]{:S(2)}) collective-permute-start(f32[128,1]{1,0:T(8,128)S(1)} %slice.2012), channel_id=1, source_target_pairs={{0,1},{1,2},{2,3},{3,4},{4,5},{5,6},{6,7},{7,8},{8,9},{9,10},{10,1... | collective-permute-start | bytes 1544 | tf_op jit(solution)/shard_map/ppermute | solution.py:37
  211.4 4.3 %collective-permute-start.27 = (f32[1,256]{1,0:T(1,128)S(1)}, f32[1,256]{1,0:T(1,128)S(1)}, u32[]{:S(2)}, u32[]{:S(2)}) collective-permute-start(f32[1,256]{1,0:T(1,128)S(1)} %slice.2020), channel_id=1, source_target_pairs={{0,16},{1,17},{2,18},{3,19},{4,20},{5,21},{6,22},{7,23},{8,24},{9,... | collective-permute-start | bytes 3080 | tf_op jit(solution)/shard_map/ppermute | solution.py:37
  215.9 9.6 %collective-permute-start.28 = (f32[128,1]{1,0:T(8,128)S(1)}, f32[128,1]{1,0:T(8,128)S(1)}, u32[]{:S(2)}, u32[]{:S(2)}) collective-permute-start(f32[128,1]{1,0:T(8,128)S(1)} %slice.2024), channel_id=1, source_target_pairs={{1,0},{2,1},{3,2},{4,3},{5,4},{6,5},{7,6},{8,7},{9,8},{10,9},{11,1... | collective-permute-start | bytes 1544 | tf_op jit(solution)/shard_map/ppermute | solution.py:37
  218.0 7.6 %collective-permute-start.30 = (f32[1,256]{1,0:T(1,128)S(1)}, f32[1,256]{1,0:T(1,128)S(1)}, u32[]{:S(2)}, u32[]{:S(2)}) collective-permute-start(f32[1,256]{1,0:T(1,128)S(1)} %slice.2028), channel_id=1, source_target_pairs={{16,0},{17,1},{18,2},{19,3},{20,4},{21,5},{22,6},{23,7},{24,8},{25... | collective-permute-start | bytes 3080 | tf_op jit(solution)/shard_map/ppermute | solution.py:37
  220.1 16.2 %collective-permute-start.20 = (f32[3,2,32,128]{3,2,1,0:T(8,128)S(1)}, f32[3,2,32,128]{3,2,1,0:T(8,128)S(1)}, u32[]{:S(2)}, u32[]{:S(2)}) collective-permute-start(f32[3,2,32,128]{3,2,1,0:T(8,128)S(1)} %get-tuple-element.169), channel_id=1, source_target_pairs={{0,16},{1,17},{2,18},{3,19},{4,20},{5,21},{6,22},{7,23},{8,24},{9,... | collective-permute-start | bytes 294920 | tf_op jit(solution)/shard_map/ppermute | solution.py:23
  221.4 14.9 %collective-permute-start.21 = (f32[3,2,32,128]{3,2,1,0:T(8,128)S(1)}, f32[3,2,32,128]{3,2,1,0:T(8,128)S(1)}, u32[]{:S(2)}, u32[]{:S(2)}) collective-permute-start(f32[3,2,32,128]{3,2,1,0:T(8,128)S(1)} %get-tuple-element.170), channel_id=1, source_target_pairs={{16,0},{17,1},{18,2},{19,3},{20,4},{21,5},{22,6},{23,7},{24,8},{25... | collective-permute-start | bytes 294920 | tf_op jit(solution)/shard_map/ppermute | solution.py:24
  225.8 7.4 %collective-permute-start.29 = (f32[128,1]{1,0:T(8,128)S(1)}, f32[128,1]{1,0:T(8,128)S(1)}, u32[]{:S(2)}, u32[]{:S(2)}) collective-permute-start(f32[128,1]{1,0:T(8,128)S(1)} %slice.2025), channel_id=1, source_target_pairs={{0,1},{1,2},{2,3},{3,4},{4,5},{5,6},{6,7},{7,8},{8,9},{9,10},{10,1... | collective-permute-start | bytes 1544 | tf_op jit(solution)/shard_map/ppermute | solution.py:37
  231.2 4.3 %collective-permute-start.31 = (f32[1,256]{1,0:T(1,128)S(1)}, f32[1,256]{1,0:T(1,128)S(1)}, u32[]{:S(2)}, u32[]{:S(2)}) collective-permute-start(f32[1,256]{1,0:T(1,128)S(1)} %slice.2029), channel_id=1, source_target_pairs={{0,16},{1,17},{2,18},{3,19},{4,20},{5,21},{6,22},{7,23},{8,24},{9,... | collective-permute-start | bytes 3080 | tf_op jit(solution)/shard_map/ppermute | solution.py:37
  236.3 5.5 %collective-permute-start.22 = (f32[3,20,2,128]{3,2,1,0:T(2,128)S(1)}, f32[3,20,2,128]{3,2,1,0:T(2,128)S(1)}, u32[]{:S(2)}, u32[]{:S(2)}) collective-permute-start(f32[3,20,2,128]{3,2,1,0:T(2,128)S(1)} %get-tuple-element.150), channel_id=1, source_target_pairs={{0,1},{1,2},{2,3},{3,4},{4,5},{5,6},{6,7},{7,8},{8,9},{9,10},{10,1... | collective-permute-start | bytes 184328 | tf_op jit(solution)/shard_map/ppermute | solution.py:23
  239.5 6.6 %collective-permute-start.23 = (f32[3,20,2,128]{3,2,1,0:T(2,128)S(1)}, f32[3,20,2,128]{3,2,1,0:T(2,128)S(1)}, u32[]{:S(2)}, u32[]{:S(2)}) collective-permute-start(f32[3,20,2,128]{3,2,1,0:T(2,128)S(1)} %get-tuple-element.151), channel_id=1, source_target_pairs={{1,0},{2,1},{3,2},{4,3},{5,4},{6,5},{7,6},{8,7},{9,8},{10,9},{11,1... | collective-permute-start | bytes 184328 | tf_op jit(solution)/shard_map/ppermute | solution.py:24
  (64 other events, 339.4 us)
where the time goes:
time: 254 us; the launch traced here: 251 us
  starting transfers between devices  91.2 us (36%)
  other arithmetic  72.3 us (28%)
  local copies, waits for them, and re-layouts  39.5 us (16%)
  waiting for transfers between devices  21.9 us (9%)
  matrix products  16.4 us (6%)
  blocking collectives  7.31 us (3%)
    ppermute x12, starting transfers between devices, extended(): after = lax.ppermute(leading, axis, down)  37.7 us
    ppermute x12, starting transfers between devices, extended(): before = lax.ppermute(last, axis, up)  30.5 us
    ppermute x8, starting transfers between devices, passed_along(): return lax.ppermute(x, axis, pairs)  23 us
    dot_general x16, matrix products, one_block(): jnp.einsum('rck,kn->rcn', onehot, table, precision=lax.Precision.HIGHEST)  16.4 us
    ppermute x12, waiting for transfers between devices, extended(): after = lax.ppermute(leading, axis, down)  15.4 us
    select_n x16, other arithmetic, one_block(): lower = indices % tile_cols  11.3 us
    select_n x16, other arithmetic, one_block(): upper = indices // tile_cols  11.3 us
    add x2, other arithmetic, per_device(): forces[5] + time_step * (lame * spread + 2.0 * shear * strain_y)  11.2 us
  transfers between devices with their start and end apart: 32, of which 11 were waited for; matrix products, arithmetic and copies ran while one was open for 10% of the time, Pallas kernels for 0%

commit v1 on v0

--- a/solution.py
+++ b/solution.py
@@ -28,7 +28,12 @@
 
 def broadcast(x, axis, root):
     mine = lax.axis_index(axis) == root
-    return lax.psum(jnp.where(mine, x, jnp.zeros_like(x)), axis)
+
+    def scan_windows(arr):
+        low = lax.all_gather(arr, axis).sum(axis=0)
+        return low
+
+    return scan_windows(jnp.where(mine, x, jnp.zeros_like(x)))
 
 
 def passed_along(x, axis, by):

time: 254 us -> 250 us (0.984)
  blocking collectives: 7.31 us -> 4.15 us
    psum x1 -> x0, blocking collectives: 7.31 us -> none  [broadcast(): return lax.psum(jnp.where(mine, x, jnp.zeros_like(x)), axis)]
    all_gather x0 -> x1, blocking collectives: none -> 4.15 us  [scan_windows(): low = lax.all_gather(arr, axis).sum(axis=0)]
    unnamed x128 -> x122, local copies, waits for them, and re-layouts: 5.89 us -> 5.83 us
where the time goes in v1:
time: 250 us; the launch traced here: 247 us
  starting transfers between devices  91.3 us (37%)
  other arithmetic  72.2 us (29%)
  local copies, waits for them, and re-layouts  38 us (15%)
  waiting for transfers between devices  22 us (9%)
  matrix products  16.4 us (7%)
  blocking collectives  4.15 us (2%)
    ppermute x12, starting transfers between devices, extended(): after = lax.ppermute(leading, axis, down)  37.1 us
    ppermute x12, starting transfers between devices, extended(): before = lax.ppermute(last, axis, up)  30.5 us
    ppermute x8, starting transfers between devices, passed_along(): return lax.ppermute(x, axis, pairs)  23.8 us
    dot_general x16, matrix products, one_block(): jnp.einsum('rck,kn->rcn', onehot, table, precision=lax.Precision.HIGHEST)  16.4 us
    ppermute x12, waiting for transfers between devices, extended(): after = lax.ppermute(leading, axis, down)  15.5 us
    select_n x16, other arithmetic, one_block(): lower = indices % tile_cols  11.3 us
    select_n x16, other arithmetic, one_block(): upper = indices // tile_cols  11.3 us
    add x2, other arithmetic, per_device(): forces[5] + time_step * (lame * spread + 2.0 * shear * strain_y)  11 us
  transfers between devices with their start and end apart: 32, of which 11 were waited for; matrix products, arithmetic and copies ran while one was open for 10% of the time, Pallas kernels for 0%

profile of v1, /device:TPU:7, one launch (start us, length us, event | category | flops | bytes accessed | tf_op | source)
XLA Modules:
  0.0 246.7 jit_solution(6693777967262925130)
XLA Ops:
  1.7 3.7 %collective-permute-start = (f32[3,16,2,128]{3,2,1,0:T(2,128)S(1)}, f32[3,16,2,128]{3,2,1,0:T(2,128)}, u32[]{:S(2)}, u32[]{:S(2)}) collective-permute-start(f32[3,16,2,128]{3,2,1,0:T(2,128)S(1)} %get-tuple-element.138), channel_id=1, source_target_pairs={{0,1},{1,2},{2,3},{3,4},{4,5},{5,6},{6,7},{7,8},{8,9},{9,10},{10,1... | collective-permute-start | bytes 147464 | tf_op jit(solution)/shard_map/ppermute | solution.py:23
  5.4 1.9 collective-permute-start.1
  10.2 4.1 %collective-permute-start.3 = (f32[3,2,32,128]{3,2,1,0:T(8,128)S(1)}, f32[3,2,32,128]{3,2,1,0:T(8,128)S(1)}, u32[]{:S(2)}, u32[]{:S(2)}) collective-permute-start(f32[3,2,32,128]{3,2,1,0:T(8,128)S(1)} %get-tuple-element.143), channel_id=1, source_target_pairs={{16,0},{17,1},{18,2},{19,3},{20,4},{21,5},{22,6},{23,7},{24,8},{25... | collective-permute-start | bytes 294920 | tf_op jit(solution)/shard_map/ppermute | solution.py:24
  29.1 6.5 %fusion.30 = (f32[16,32,128]{2,1,0:T(8,128)S(1)}, f32[16,32,128]{2,1,0:T(8,128)S(1)}, pred[16,32,128]{2,1,0:T(8,128)(4,1)S(1)}, pred[16,32,128]{2,1,0:T(8,128)(4...) fusion(f32[3,16,32,128]{3,2,1,0:T(8,128)S(1)} %copy-done.1, ...), kind=kLoop, calls=%fused_computation.102 | loop fusion | flops 3211264 | bytes 4915232 | tf_op jit(solution)/shard_map/add | solution.py:130
  39.3 4.0 %collective-permute-start.5 = (f32[3,2,32,128]{3,2,1,0:T(8,128)S(1)}, f32[3,2,32,128]{3,2,1,0:T(8,128)S(1)}, u32[]{:S(2)}, u32[]{:S(2)}) collective-permute-start(f32[3,2,32,128]{3,2,1,0:T(8,128)S(1)} %get-tuple-element.190), channel_id=1, source_target_pairs={{16,0},{17,1},{18,2},{19,3},{20,4},{21,5},{22,6},{23,7},{24,8},{25... | collective-permute-start | bytes 294920 | tf_op jit(solution)/shard_map/ppermute | solution.py:24
  45.0 6.2 %collective-permute-start.6 = (f32[3,20,2,128]{3,2,1,0:T(2,128)S(1)}, f32[3,20,2,128]{3,2,1,0:T(2,128)S(1)}, u32[]{:S(2)}, u32[]{:S(2)}) collective-permute-start(f32[3,20,2,128]{3,2,1,0:T(2,128)S(1)} %get-tuple-element.160), channel_id=1, source_target_pairs={{0,1},{1,2},{2,3},{3,4},{4,5},{5,6},{6,7},{7,8},{8,9},{9,10},{10,1... | collective-permute-start | bytes 184328 | tf_op jit(solution)/shard_map/ppermute | solution.py:23
  51.3 1.9 collective-permute-start.7
  53.4 4.2 %collective-permute-done.7 = f32[3,20,2,128]{3,2,1,0:T(2,128)S(1)} collective-permute-done((f32[3,20,2,128]{3,2,1,0:T(2,128)S(1)}, f32[3,20,2,128]{3,2,1,0:T(2,128)S(1)}, u32[]{:S(2)}, u32[]{:S(2)}) %collective-permute-start.7) | collective-permute-done | bytes 61472 | tf_op jit(solution)/shard_map/ppermute | solution.py:24
  57.8 10.7 %multiply_add_fusion.3 = (f32[16,32,128]{2,1,0:T(8,128)S(1)}, f32[16,32,128]{2,1,0:T(8,128)S(1)}, f32[16,32,128]{2,1,0:T(8,128)S(1)}, f32[16,32,128]{2,1,0:T(8,1...) fusion(f32[6,16,32,128]{3,2,1,0:T(8,128)S(1)} %copy-done, ...), kind=kLoop, calls=%fused_computation.482 | loop fusion | flops 3670016 | bytes 5505088 | tf_op jit(solution)/shard_map/add | solution.py:160
  70.5 1.9 collective-permute-start.8
  72.5 2.4 collective-permute-start.9
  76.6 4.0 %collective-permute-start.11 = (f32[3,2,32,128]{3,2,1,0:T(8,128)S(1)}, f32[3,2,32,128]{3,2,1,0:T(8,128)S(1)}, u32[]{:S(2)}, u32[]{:S(2)}) collective-permute-start(f32[3,2,32,128]{3,2,1,0:T(8,128)S(1)} %get-tuple-element.185), channel_id=1, source_target_pairs={{16,0},{17,1},{18,2},{19,3},{20,4},{21,5},{22,6},{23,7},{24,8},{25... | collective-permute-start | bytes 294920 | tf_op jit(solution)/shard_map/ppermute | solution.py:24
  86.0 4.1 %collective-permute-start.13 = (f32[3,2,32,128]{3,2,1,0:T(8,128)S(1)}, f32[3,2,32,128]{3,2,1,0:T(8,128)S(1)}, u32[]{:S(2)}, u32[]{:S(2)}) collective-permute-start(f32[3,2,32,128]{3,2,1,0:T(8,128)S(1)} %get-tuple-element.180), channel_id=1, source_target_pairs={{16,0},{17,1},{18,2},{19,3},{20,4},{21,5},{22,6},{23,7},{24,8},{25... | collective-permute-start | bytes 294920 | tf_op jit(solution)/shard_map/ppermute | solution.py:24
  91.8 5.9 %collective-permute-start.14 = (f32[3,20,2,128]{3,2,1,0:T(2,128)S(1)}, f32[3,20,2,128]{3,2,1,0:T(2,128)S(1)}, u32[]{:S(2)}, u32[]{:S(2)}) collective-permute-start(f32[3,20,2,128]{3,2,1,0:T(2,128)S(1)} %get-tuple-element.155), channel_id=1, source_target_pairs={{0,1},{1,2},{2,3},{3,4},{4,5},{5,6},{6,7},{7,8},{8,9},{9,10},{10,1... | collective-permute-start | bytes 184328 | tf_op jit(solution)/shard_map/ppermute | solution.py:23
  97.7 2.1 collective-permute-start.15
  101.0 3.1 %collective-permute-done.15 = f32[3,20,2,128]{3,2,1,0:T(2,128)S(1)} collective-permute-done((f32[3,20,2,128]{3,2,1,0:T(2,128)S(1)}, f32[3,20,2,128]{3,2,1,0:T(2,128)S(1)}, u32[]{:S(2)}, u32[]{:S(2)}) %collective-permute-start.15) | collective-permute-done | bytes 61472 | tf_op jit(solution)/shard_map/ppermute | solution.py:24
  111.0 2.4 collective-permute-start.17
  116.4 4.0 %collective-permute-start.19 = (f32[3,2,32,128]{3,2,1,0:T(8,128)S(1)}, f32[3,2,32,128]{3,2,1,0:T(8,128)S(1)}, u32[]{:S(2)}, u32[]{:S(2)}) collective-permute-start(f32[3,2,32,128]{3,2,1,0:T(8,128)S(1)} %get-tuple-element.175), channel_id=1, source_target_pairs={{16,0},{17,1},{18,2},{19,3},{20,4},{21,5},{22,6},{23,7},{24,8},{25... | collective-permute-start | bytes 294920 | tf_op jit(solution)/shard_map/ppermute | solution.py:24
  123.8 4.2 %all_gather.4 = f32[2,2,32,128]{3,2,1,0:T(8,128)S(1)} all-gather(f32[1,2,32,128]{3,2,1,0:T(8,128)S(1)} %maximum_select_fusion), channel_id=1, replica_groups=mesh['depth'=2,'map'=16] {'depth'}, dimensions={0}, use_global_device_ids=true | all-gather | bytes 98304 | tf_op jit(solution)/shard_map/all_gather | solution.py:33
  128.0 52.3 %while.13 = (s32[]{:T(128)}, f32[16,2,8,256]{3,2,1,0:T(8,128)}, s32[16,8,256]{2,1,0:T(8,128)}, f32[32,256]{1,0:T(8,128)S(1)}, s32[]{:T(128)}) while((s32[]{:T(128)}, f32[16,2,8,256]{3,2,1,0:T(8,128)}, s32[16,8,256]{2,1,0:T(8,128)}, f32[32,256]{1,0:T(8,128)S(1)}, s32[]{:T(128)}) %tuple.162), condition=%wide.region_4.5_spmd.clone, body=%wide.region_1.4_spmd.clone.sunk | while | flops 202754048 | bytes 4330053 | solution.py:103
  181.4 2.0 fusion.105
  190.1 3.9 %collective-permute-start.24 = (f32[2,128,1]{1,2,0:T(1,128)S(1)}, f32[2,128,1]{1,2,0:T(1,128)S(1)}, u32[]{:S(2)}, u32[]{:S(2)}) collective-permute-start(f32[2,128,1]{1,2,0:T(1,128)S(1)} %pad_maximum_fusion.64), channel_id=1, source_target_pairs={{1,0},{2,1},{3,2},{4,3},{5,4},{6,5},{7,6},{8,7},{9,8},{10,9},{11,1... | collective-permute-start | bytes 3080 | tf_op jit(solution)/shard_map/ppermute | solution.py:42
  194.8 3.6 %collective-permute-start.26 = (f32[2,1,256]{2,1,0:T(1,128)S(1)}, f32[2,1,256]{2,1,0:T(1,128)S(1)}, u32[]{:S(2)}, u32[]{:S(2)}) collective-permute-start(f32[2,1,256]{2,1,0:T(1,128)S(1)} %pad_maximum_fusion.63), channel_id=1, source_target_pairs={{16,0},{17,1},{18,2},{19,3},{20,4},{21,5},{22,6},{23,7},{24,8},{25... | collective-permute-start | bytes 6152 | tf_op jit(solution)/shard_map/ppermute | solution.py:42
  200.7 4.6 %collective-permute-start.25 = (f32[128,1]{1,0:T(8,128)S(1)}, f32[128,1]{1,0:T(8,128)S(1)}, u32[]{:S(2)}, u32[]{:S(2)}) collective-permute-start(f32[128,1]{1,0:T(8,128)S(1)} %slice.2012), channel_id=1, source_target_pairs={{0,1},{1,2},{2,3},{3,4},{4,5},{5,6},{6,7},{7,8},{8,9},{9,10},{10,1... | collective-permute-start | bytes 1544 | tf_op jit(solution)/shard_map/ppermute | solution.py:42
  206.6 2.9 %collective-permute-done.27 = f32[1,256]{1,0:T(1,128)S(1)} collective-permute-done((f32[1,256]{1,0:T(1,128)S(1)}, f32[1,256]{1,0:T(1,128)S(1)}, u32[]{:S(2)}, u32[]{:S(2)}) %collective-permute-start.27) | collective-permute-done | bytes 1056 | tf_op jit(solution)/shard_map/ppermute | solution.py:42
  210.6 2.1 collective-permute-start.28
  216.1 4.0 %collective-permute-start.21 = (f32[3,2,32,128]{3,2,1,0:T(8,128)S(1)}, f32[3,2,32,128]{3,2,1,0:T(8,128)S(1)}, u32[]{:S(2)}, u32[]{:S(2)}) collective-permute-start(f32[3,2,32,128]{3,2,1,0:T(8,128)S(1)} %get-tuple-element.170), channel_id=1, source_target_pairs={{16,0},{17,1},{18,2},{19,3},{20,4},{21,5},{22,6},{23,7},{24,8},{25... | collective-permute-start | bytes 294920 | tf_op jit(solution)/shard_map/ppermute | solution.py:24
  220.5 5.4 %collective-permute-start.29 = (f32[128,1]{1,0:T(8,128)S(1)}, f32[128,1]{1,0:T(8,128)S(1)}, u32[]{:S(2)}, u32[]{:S(2)}) collective-permute-start(f32[128,1]{1,0:T(8,128)S(1)} %slice.2025), channel_id=1, source_target_pairs={{0,1},{1,2},{2,3},{3,4},{4,5},{5,6},{6,7},{7,8},{8,9},{9,10},{10,1... | collective-permute-start | bytes 1544 | tf_op jit(solution)/shard_map/ppermute | solution.py:42
  227.9 2.3 collective-permute-done.31
  231.9 3.1 %collective-permute-start.22 = (f32[3,20,2,128]{3,2,1,0:T(2,128)S(1)}, f32[3,20,2,128]{3,2,1,0:T(2,128)S(1)}, u32[]{:S(2)}, u32[]{:S(2)}) collective-permute-start(f32[3,20,2,128]{3,2,1,0:T(2,128)S(1)} %get-tuple-element.150), channel_id=1, source_target_pairs={{0,1},{1,2},{2,3},{3,4},{4,5},{5,6},{6,7},{7,8},{8,9},{9,10},{10,1... | collective-permute-start | bytes 184328 | tf_op jit(solution)/shard_map/ppermute | solution.py:23
  235.0 2.1 collective-permute-start.23
  237.4 4.2 %collective-permute-done.23 = f32[3,20,2,128]{3,2,1,0:T(2,128)S(1)} collective-permute-done((f32[3,20,2,128]{3,2,1,0:T(2,128)S(1)}, f32[3,20,2,128]{3,2,1,0:T(2,128)S(1)}, u32[]{:S(2)}, u32[]{:S(2)}) %collective-permute-start.23) | collective-permute-done | bytes 61472 | tf_op jit(solution)/shard_map/ppermute | solution.py:24
  (380 shorter events, 126.5 us)
Async XLA Ops:
  1.7 25.1 %collective-permute-start = (f32[3,16,2,128]{3,2,1,0:T(2,128)S(1)}, f32[3,16,2,128]{3,2,1,0:T(2,128)}, u32[]{:S(2)}, u32[]{:S(2)}) collective-permute-start(f32[3,16,2,128]{3,2,1,0:T(2,128)S(1)} %get-tuple-element.138), channel_id=1, source_target_pairs={{0,1},{1,2},{2,3},{3,4},{4,5},{5,6},{6,7},{7,8},{8,9},{9,10},{10,1... | collective-permute-start | bytes 147464 | tf_op jit(solution)/shard_map/ppermute | solution.py:23
  5.4 21.4 %collective-permute-start.1 = (f32[3,16,2,128]{3,2,1,0:T(2,128)S(1)}, f32[3,16,2,128]{3,2,1,0:T(2,128)}, u32[]{:S(2)}, u32[]{:S(2)}) collective-permute-start(f32[3,16,2,128]{3,2,1,0:T(2,128)S(1)} %get-tuple-element.139), channel_id=1, source_target_pairs={{1,0},{2,1},{3,2},{4,3},{5,4},{6,5},{7,6},{8,7},{9,8},{10,9},{11,1... | collective-permute-start | bytes 147464 | tf_op jit(solution)/shard_map/ppermute | solution.py:24
  8.9 19.4 %collective-permute-start.2 = (f32[3,2,32,128]{3,2,1,0:T(8,128)}, f32[3,2,32,128]{3,2,1,0:T(8,128)S(1)}, u32[]{:S(2)}, u32[]{:S(2)}) collective-permute-start(f32[3,2,32,128]{3,2,1,0:T(8,128)} %get-tuple-element.142), channel_id=1, source_target_pairs={{0,16},{1,17},{2,18},{3,19},{4,20},{5,21},{6,22},{7,23},{8,24},{9,... | collective-permute-start | bytes 294920 | tf_op jit(solution)/shard_map/ppermute | solution.py:23
  10.2 18.1 %collective-permute-start.3 = (f32[3,2,32,128]{3,2,1,0:T(8,128)S(1)}, f32[3,2,32,128]{3,2,1,0:T(8,128)S(1)}, u32[]{:S(2)}, u32[]{:S(2)}) collective-permute-start(f32[3,2,32,128]{3,2,1,0:T(8,128)S(1)} %get-tuple-element.143), channel_id=1, source_target_pairs={{16,0},{17,1},{18,2},{19,3},{20,4},{21,5},{22,6},{23,7},{24,8},{25... | collective-permute-start | bytes 294920 | tf_op jit(solution)/shard_map/ppermute | solution.py:24
  38.0 5.9 %collective-permute-start.4 = (f32[3,2,32,128]{3,2,1,0:T(8,128)S(1)}, f32[3,2,32,128]{3,2,1,0:T(8,128)S(1)}, u32[]{:S(2)}, u32[]{:S(2)}) collective-permute-start(f32[3,2,32,128]{3,2,1,0:T(8,128)S(1)} %get-tuple-element.189), channel_id=1, source_target_pairs={{0,16},{1,17},{2,18},{3,19},{4,20},{5,21},{6,22},{7,23},{8,24},{9,... | collective-permute-start | bytes 294920 | tf_op jit(solution)/shard_map/ppermute | solution.py:23
  39.3 5.6 %collective-permute-start.5 = (f32[3,2,32,128]{3,2,1,0:T(8,128)S(1)}, f32[3,2,32,128]{3,2,1,0:T(8,128)S(1)}, u32[]{:S(2)}, u32[]{:S(2)}) collective-permute-start(f32[3,2,32,128]{3,2,1,0:T(8,128)S(1)} %get-tuple-element.190), channel_id=1, source_target_pairs={{16,0},{17,1},{18,2},{19,3},{20,4},{21,5},{22,6},{23,7},{24,8},{25... | collective-permute-start | bytes 294920 | tf_op jit(solution)/shard_map/ppermute | solution.py:24
  45.0 8.4 %collective-permute-start.6 = (f32[3,20,2,128]{3,2,1,0:T(2,128)S(1)}, f32[3,20,2,128]{3,2,1,0:T(2,128)S(1)}, u32[]{:S(2)}, u32[]{:S(2)}) collective-permute-start(f32[3,20,2,128]{3,2,1,0:T(2,128)S(1)} %get-tuple-element.160), channel_id=1, source_target_pairs={{0,1},{1,2},{2,3},{3,4},{4,5},{5,6},{6,7},{7,8},{8,9},{9,10},{10,1... | collective-permute-start | bytes 184328 | tf_op jit(solution)/shard_map/ppermute | solution.py:23
  51.3 6.4 %collective-permute-start.7 = (f32[3,20,2,128]{3,2,1,0:T(2,128)S(1)}, f32[3,20,2,128]{3,2,1,0:T(2,128)S(1)}, u32[]{:S(2)}, u32[]{:S(2)}) collective-permute-start(f32[3,20,2,128]{3,2,1,0:T(2,128)S(1)} %get-tuple-element.161), channel_id=1, source_target_pairs={{1,0},{2,1},{3,2},{4,3},{5,4},{6,5},{7,6},{8,7},{9,8},{10,9},{11,1... | collective-permute-start | bytes 184328 | tf_op jit(solution)/shard_map/ppermute | solution.py:24
  70.5 10.1 %collective-permute-start.8 = (f32[3,16,2,128]{3,2,1,0:T(2,128)S(1)}, f32[3,16,2,128]{3,2,1,0:T(2,128)S(1)}, u32[]{:S(2)}, u32[]{:S(2)}) collective-permute-start(f32[3,16,2,128]{3,2,1,0:T(2,128)S(1)} %get-tuple-element.181), channel_id=1, source_target_pairs={{0,1},{1,2},{2,3},{3,4},{4,5},{5,6},{6,7},{7,8},{8,9},{9,10},{10,1... | collective-permute-start | bytes 147464 | tf_op jit(solution)/shard_map/ppermute | solution.py:23
  72.5 8.2 %collective-permute-start.9 = (f32[3,16,2,128]{3,2,1,0:T(2,128)S(1)}, f32[3,16,2,128]{3,2,1,0:T(2,128)S(1)}, u32[]{:S(2)}, u32[]{:S(2)}) collective-permute-start(f32[3,16,2,128]{3,2,1,0:T(2,128)S(1)} %get-tuple-element.182), channel_id=1, source_target_pairs={{1,0},{2,1},{3,2},{4,3},{5,4},{6,5},{7,6},{8,7},{9,8},{10,9},{11,1... | collective-permute-start | bytes 147464 | tf_op jit(solution)/shard_map/ppermute | solution.py:24
  75.3 6.3 %collective-permute-start.10 = (f32[3,2,32,128]{3,2,1,0:T(8,128)S(1)}, f32[3,2,32,128]{3,2,1,0:T(8,128)S(1)}, u32[]{:S(2)}, u32[]{:S(2)}) collective-permute-start(f32[3,2,32,128]{3,2,1,0:T(8,128)S(1)} %get-tuple-element.186), channel_id=1, source_target_pairs={{0,16},{1,17},{2,18},{3,19},{4,20},{5,21},{6,22},{7,23},{8,24},{9,... | collective-permute-start | bytes 294920 | tf_op jit(solution)/shard_map/ppermute | solution.py:23
  76.6 5.9 %collective-permute-start.11 = (f32[3,2,32,128]{3,2,1,0:T(8,128)S(1)}, f32[3,2,32,128]{3,2,1,0:T(8,128)S(1)}, u32[]{:S(2)}, u32[]{:S(2)}) collective-permute-start(f32[3,2,32,128]{3,2,1,0:T(8,128)S(1)} %get-tuple-element.185), channel_id=1, source_target_pairs={{16,0},{17,1},{18,2},{19,3},{20,4},{21,5},{22,6},{23,7},{24,8},{25... | collective-permute-start | bytes 294920 | tf_op jit(solution)/shard_map/ppermute | solution.py:24
  84.7 6.0 %collective-permute-start.12 = (f32[3,2,32,128]{3,2,1,0:T(8,128)S(1)}, f32[3,2,32,128]{3,2,1,0:T(8,128)S(1)}, u32[]{:S(2)}, u32[]{:S(2)}) collective-permute-start(f32[3,2,32,128]{3,2,1,0:T(8,128)S(1)} %get-tuple-element.179), channel_id=1, source_target_pairs={{0,16},{1,17},{2,18},{3,19},{4,20},{5,21},{6,22},{7,23},{8,24},{9,... | collective-permute-start | bytes 294920 | tf_op jit(solution)/shard_map/ppermute | solution.py:23
  86.0 5.7 %collective-permute-start.13 = (f32[3,2,32,128]{3,2,1,0:T(8,128)S(1)}, f32[3,2,32,128]{3,2,1,0:T(8,128)S(1)}, u32[]{:S(2)}, u32[]{:S(2)}) collective-permute-start(f32[3,2,32,128]{3,2,1,0:T(8,128)S(1)} %get-tuple-element.180), channel_id=1, source_target_pairs={{16,0},{17,1},{18,2},{19,3},{20,4},{21,5},{22,6},{23,7},{24,8},{25... | collective-permute-start | bytes 294920 | tf_op jit(solution)/shard_map/ppermute | solution.py:24
  91.8 9.3 %collective-permute-start.14 = (f32[3,20,2,128]{3,2,1,0:T(2,128)S(1)}, f32[3,20,2,128]{3,2,1,0:T(2,128)S(1)}, u32[]{:S(2)}, u32[]{:S(2)}) collective-permute-start(f32[3,20,2,128]{3,2,1,0:T(2,128)S(1)} %get-tuple-element.155), channel_id=1, source_target_pairs={{0,1},{1,2},{2,3},{3,4},{4,5},{5,6},{6,7},{7,8},{8,9},{9,10},{10,1... | collective-permute-start | bytes 184328 | tf_op jit(solution)/shard_map/ppermute | solution.py:23
  97.7 6.4 %collective-permute-start.15 = (f32[3,20,2,128]{3,2,1,0:T(2,128)S(1)}, f32[3,20,2,128]{3,2,1,0:T(2,128)S(1)}, u32[]{:S(2)}, u32[]{:S(2)}) collective-permute-start(f32[3,20,2,128]{3,2,1,0:T(2,128)S(1)} %get-tuple-element.156), channel_id=1, source_target_pairs={{1,0},{2,1},{3,2},{4,3},{5,4},{6,5},{7,6},{8,7},{9,8},{10,9},{11,1... | collective-permute-start | bytes 184328 | tf_op jit(solution)/shard_map/ppermute | solution.py:24
  109.1 11.4 %collective-permute-start.16 = (f32[3,16,2,128]{3,2,1,0:T(2,128)S(1)}, f32[3,16,2,128]{3,2,1,0:T(2,128)S(1)}, u32[]{:S(2)}, u32[]{:S(2)}) collective-permute-start(f32[3,16,2,128]{3,2,1,0:T(2,128)S(1)} %get-tuple-element.171), channel_id=1, source_target_pairs={{0,1},{1,2},{2,3},{3,4},{4,5},{5,6},{6,7},{7,8},{8,9},{9,10},{10,1... | collective-permute-start | bytes 147464 | tf_op jit(solution)/shard_map/ppermute | solution.py:23
  111.0 9.5 %collective-permute-start.17 = (f32[3,16,2,128]{3,2,1,0:T(2,128)S(1)}, f32[3,16,2,128]{3,2,1,0:T(2,128)S(1)}, u32[]{:S(2)}, u32[]{:S(2)}) collective-permute-start(f32[3,16,2,128]{3,2,1,0:T(2,128)S(1)} %get-tuple-element.172), channel_id=1, source_target_pairs={{1,0},{2,1},{3,2},{4,3},{5,4},{6,5},{7,6},{8,7},{9,8},{10,9},{11,1... | collective-permute-start | bytes 147464 | tf_op jit(solution)/shard_map/ppermute | solution.py:24
  115.1 6.3 %collective-permute-start.18 = (f32[3,2,32,128]{3,2,1,0:T(8,128)S(1)}, f32[3,2,32,128]{3,2,1,0:T(8,128)S(1)}, u32[]{:S(2)}, u32[]{:S(2)}) collective-permute-start(f32[3,2,32,128]{3,2,1,0:T(8,128)S(1)} %get-tuple-element.176), channel_id=1, source_target_pairs={{0,16},{1,17},{2,18},{3,19},{4,20},{5,21},{6,22},{7,23},{8,24},{9,... | collective-permute-start | bytes 294920 | tf_op jit(solution)/shard_map/ppermute | solution.py:23
  116.4 5.9 %collective-permute-start.19 = (f32[3,2,32,128]{3,2,1,0:T(8,128)S(1)}, f32[3,2,32,128]{3,2,1,0:T(8,128)S(1)}, u32[]{:S(2)}, u32[]{:S(2)}) collective-permute-start(f32[3,2,32,128]{3,2,1,0:T(8,128)S(1)} %get-tuple-element.175), channel_id=1, source_target_pairs={{16,0},{17,1},{18,2},{19,3},{20,4},{21,5},{22,6},{23,7},{24,8},{25... | collective-permute-start | bytes 294920 | tf_op jit(solution)/shard_map/ppermute | solution.py:24
  190.1 8.3 %collective-permute-start.24 = (f32[2,128,1]{1,2,0:T(1,128)S(1)}, f32[2,128,1]{1,2,0:T(1,128)S(1)}, u32[]{:S(2)}, u32[]{:S(2)}) collective-permute-start(f32[2,128,1]{1,2,0:T(1,128)S(1)} %pad_maximum_fusion.64), channel_id=1, source_target_pairs={{1,0},{2,1},{3,2},{4,3},{5,4},{6,5},{7,6},{8,7},{9,8},{10,9},{11,1... | collective-permute-start | bytes 3080 | tf_op jit(solution)/shard_map/ppermute | solution.py:42
  194.8 4.4 %collective-permute-start.26 = (f32[2,1,256]{2,1,0:T(1,128)S(1)}, f32[2,1,256]{2,1,0:T(1,128)S(1)}, u32[]{:S(2)}, u32[]{:S(2)}) collective-permute-start(f32[2,1,256]{2,1,0:T(1,128)S(1)} %pad_maximum_fusion.63), channel_id=1, source_target_pairs={{16,0},{17,1},{18,2},{19,3},{20,4},{21,5},{22,6},{23,7},{24,8},{25... | collective-permute-start | bytes 6152 | tf_op jit(solution)/shard_map/ppermute | solution.py:42
  200.7 5.9 %collective-permute-start.25 = (f32[128,1]{1,0:T(8,128)S(1)}, f32[128,1]{1,0:T(8,128)S(1)}, u32[]{:S(2)}, u32[]{:S(2)}) collective-permute-start(f32[128,1]{1,0:T(8,128)S(1)} %slice.2012), channel_id=1, source_target_pairs={{0,1},{1,2},{2,3},{3,4},{4,5},{5,6},{6,7},{7,8},{8,9},{9,10},{10,1... | collective-permute-start | bytes 1544 | tf_op jit(solution)/shard_map/ppermute | solution.py:42
  205.2 4.3 %collective-permute-start.27 = (f32[1,256]{1,0:T(1,128)S(1)}, f32[1,256]{1,0:T(1,128)S(1)}, u32[]{:S(2)}, u32[]{:S(2)}) collective-permute-start(f32[1,256]{1,0:T(1,128)S(1)} %slice.2020), channel_id=1, source_target_pairs={{0,16},{1,17},{2,18},{3,19},{4,20},{5,21},{6,22},{7,23},{8,24},{9,... | collective-permute-start | bytes 3080 | tf_op jit(solution)/shard_map/ppermute | solution.py:42
  210.6 9.6 %collective-permute-start.28 = (f32[128,1]{1,0:T(8,128)S(1)}, f32[128,1]{1,0:T(8,128)S(1)}, u32[]{:S(2)}, u32[]{:S(2)}) collective-permute-start(f32[128,1]{1,0:T(8,128)S(1)} %slice.2024), channel_id=1, source_target_pairs={{1,0},{2,1},{3,2},{4,3},{5,4},{6,5},{7,6},{8,7},{9,8},{10,9},{11,1... | collective-permute-start | bytes 1544 | tf_op jit(solution)/shard_map/ppermute | solution.py:42
  212.7 7.6 %collective-permute-start.30 = (f32[1,256]{1,0:T(1,128)S(1)}, f32[1,256]{1,0:T(1,128)S(1)}, u32[]{:S(2)}, u32[]{:S(2)}) collective-permute-start(f32[1,256]{1,0:T(1,128)S(1)} %slice.2028), channel_id=1, source_target_pairs={{16,0},{17,1},{18,2},{19,3},{20,4},{21,5},{22,6},{23,7},{24,8},{25... | collective-permute-start | bytes 3080 | tf_op jit(solution)/shard_map/ppermute | solution.py:42
  214.8 17.1 %collective-permute-start.20 = (f32[3,2,32,128]{3,2,1,0:T(8,128)S(1)}, f32[3,2,32,128]{3,2,1,0:T(8,128)S(1)}, u32[]{:S(2)}, u32[]{:S(2)}) collective-permute-start(f32[3,2,32,128]{3,2,1,0:T(8,128)S(1)} %get-tuple-element.169), channel_id=1, source_target_pairs={{0,16},{1,17},{2,18},{3,19},{4,20},{5,21},{6,22},{7,23},{8,24},{9,... | collective-permute-start | bytes 294920 | tf_op jit(solution)/shard_map/ppermute | solution.py:23
  216.1 15.8 %collective-permute-start.21 = (f32[3,2,32,128]{3,2,1,0:T(8,128)S(1)}, f32[3,2,32,128]{3,2,1,0:T(8,128)S(1)}, u32[]{:S(2)}, u32[]{:S(2)}) collective-permute-start(f32[3,2,32,128]{3,2,1,0:T(8,128)S(1)} %get-tuple-element.170), channel_id=1, source_target_pairs={{16,0},{17,1},{18,2},{19,3},{20,4},{21,5},{22,6},{23,7},{24,8},{25... | collective-permute-start | bytes 294920 | tf_op jit(solution)/shard_map/ppermute | solution.py:24
  220.5 7.4 %collective-permute-start.29 = (f32[128,1]{1,0:T(8,128)S(1)}, f32[128,1]{1,0:T(8,128)S(1)}, u32[]{:S(2)}, u32[]{:S(2)}) collective-permute-start(f32[128,1]{1,0:T(8,128)S(1)} %slice.2025), channel_id=1, source_target_pairs={{0,1},{1,2},{2,3},{3,4},{4,5},{5,6},{6,7},{7,8},{8,9},{9,10},{10,1... | collective-permute-start | bytes 1544 | tf_op jit(solution)/shard_map/ppermute | solution.py:42
  225.8 4.3 %collective-permute-start.31 = (f32[1,256]{1,0:T(1,128)S(1)}, f32[1,256]{1,0:T(1,128)S(1)}, u32[]{:S(2)}, u32[]{:S(2)}) collective-permute-start(f32[1,256]{1,0:T(1,128)S(1)} %slice.2029), channel_id=1, source_target_pairs={{0,16},{1,17},{2,18},{3,19},{4,20},{5,21},{6,22},{7,23},{8,24},{9,... | collective-permute-start | bytes 3080 | tf_op jit(solution)/shard_map/ppermute | solution.py:42
  231.9 5.5 %collective-permute-start.22 = (f32[3,20,2,128]{3,2,1,0:T(2,128)S(1)}, f32[3,20,2,128]{3,2,1,0:T(2,128)S(1)}, u32[]{:S(2)}, u32[]{:S(2)}) collective-permute-start(f32[3,20,2,128]{3,2,1,0:T(2,128)S(1)} %get-tuple-element.150), channel_id=1, source_target_pairs={{0,1},{1,2},{2,3},{3,4},{4,5},{5,6},{6,7},{7,8},{8,9},{9,10},{10,1... | collective-permute-start | bytes 184328 | tf_op jit(solution)/shard_map/ppermute | solution.py:23
  235.0 6.6 %collective-permute-start.23 = (f32[3,20,2,128]{3,2,1,0:T(2,128)S(1)}, f32[3,20,2,128]{3,2,1,0:T(2,128)S(1)}, u32[]{:S(2)}, u32[]{:S(2)}) collective-permute-start(f32[3,20,2,128]{3,2,1,0:T(2,128)S(1)} %get-tuple-element.151), channel_id=1, source_target_pairs={{1,0},{2,1},{3,2},{4,3},{5,4},{6,5},{7,6},{8,7},{9,8},{10,9},{11,1... | collective-permute-start | bytes 184328 | tf_op jit(solution)/shard_map/ppermute | solution.py:24
  (61 other events, 326.4 us)
